TPU v7x, 256 devices: a whole 4x4x8 slice. The times are simulated.
256 devices in a mesh: wide: 32 (over y, x, core), narrow: 8 (over z).
Axes of the slice: x: 4, y: 4, z: 8, core: 2. Of those that a mesh axis runs over, the one named last changes fastest.
Arguments:
- covariates: bfloat16 [524288, 128], P(('wide', 'narrow')), may hold values from -6 to 6
- level_codes: int32 [524288], P(('wide', 'narrow')), may hold values from 0 to 3
- sign_bits: int32 [524288], P(('wide', 'narrow')), may hold values from 0 to 1
- sample_rows: int32 [1024], P(('wide', 'narrow')), may hold values from 0 to 2047, as said below
- effects: float32 [512], replicated, may hold values from -6 to 6
- noise: float32 [524288], P(('wide', 'narrow')), may hold values from -8 to 8
Outputs:
- coefficients: float32 [512], replicated
- residual: float32 [524288], P(('wide', 'narrow'))
- factor: float32 [512, 512], replicated
Inputs may be any that keep to these rules, and one draw needn't show every extreme that they name: `sample_rows`: a local row offset on the device that owns the entry.
All inputs are finite; a program needn't handle non-finite values.
Results may differ from a plain program's by a relative error of at most 0.0006.
The roundings to bfloat16 on the way count: a program that leaves them out, or rounds other values in their place, can miss the bound.
Values may be sent and summed in bfloat16 or wider, within the bound.
A program may use at most 64 MiB of HBM per device.

v0:
```python
import math
import jax
import jax.numpy as jnp
from jax import lax
from jax.sharding import PartitionSpec as P

COV = 128
LEVELS = 4
HB = 256
SKETCH = 1024
ITERS = 4
half_root = math.sqrt(0.5)


def partner(value, axis, apart):
    mask = 2**apart
    pairs = [(source, source ^ mask) for source in range(lax.axis_size(axis))]
    return lax.ppermute(value, axis, pairs)


def hadamard(size):
    left = jnp.arange(size, dtype=jnp.int32)[:, None]
    right = jnp.arange(size, dtype=jnp.int32)[None, :]
    common = jnp.bitwise_and(left, right)
    parity = jnp.zeros((size, size), jnp.int32)
    for place in range(size.bit_length()):
        parity = parity + jnp.bitwise_and(jnp.right_shift(common, place), 1)
    return (1 - 2 * (parity % 2)).astype(jnp.bfloat16)


def tri_solve(lower, vector, transpose):
    return lax.linalg.triangular_solve(
        lower, vector[:, None], left_side=True, lower=True, transpose_a=transpose
    )[:, 0]


def combine_pair(own, theirs, upper):
    own_wide = own.astype(jnp.float32)
    their_wide = theirs.astype(jnp.float32)
    low = jnp.where(upper, their_wide, own_wide)
    high = jnp.where(upper, own_wide, their_wide)
    return (jnp.where(upper, low - high, low + high) * half_root).astype(jnp.bfloat16)


def body(covariates, level_codes, sign_bits, sample_rows, effects, noise):
    rows_dev = covariates.shape[0]
    cols = LEVELS * COV
    onehot = (level_codes[:, None] == jnp.arange(LEVELS, dtype=jnp.int32)[None, :]).astype(
        jnp.float32
    )
    flipped = covariates * (1 - 2 * sign_bits).astype(jnp.bfloat16)[:, None]
    design = (onehot.astype(jnp.bfloat16)[:, :, None] * flipped[:, None, :]).reshape(
        rows_dev // HB, HB, cols
    )
    local = jnp.einsum("ij,gjc->gic", hadamard(HB), design, preferred_element_type=jnp.float32)
    local = (local * (1.0 / math.sqrt(HB))).astype(jnp.bfloat16).reshape(rows_dev, cols)
    wide_index = lax.axis_index("wide")
    mixed = local
    for place in range(3):
        upper = jnp.bitwise_and(jnp.right_shift(wide_index, place), 1) == 1
        theirs = partner(mixed, "wide", place)
        mixed = combine_pair(mixed, theirs, upper)
    sketch = mixed[sample_rows]
    gram = lax.psum(
        jnp.dot(sketch.T, sketch, preferred_element_type=jnp.float32), ("wide", "narrow")
    )
    lower = jnp.linalg.cholesky(gram)
    factor = lower.T * math.sqrt(LEVELS / SKETCH)
    wide_cov = covariates.astype(jnp.float32)

    def apply_design(vector):
        values = jnp.dot(wide_cov, vector.reshape(LEVELS, COV).T, precision=lax.Precision.HIGHEST)
        return jnp.sum(values * onehot, axis=1)

    def adjoint(vector):
        return jnp.dot(
            (onehot * vector[:, None]).T, wide_cov, precision=lax.Precision.HIGHEST
        ).reshape(cols)

    resid = apply_design(effects) + noise
    gradient_now = lax.psum(adjoint(resid), ("wide", "narrow"))
    steer = tri_solve(lower, gradient_now, False)
    direction = steer
    gamma = jnp.sum(steer * steer)
    solved = jnp.zeros((cols,), jnp.float32)
    for step in range(ITERS):
        image = apply_design(tri_solve(lower, direction, True))
        alpha = gamma / lax.psum(jnp.sum(image * image), ("wide", "narrow"))
        solved = solved + alpha * direction
        resid = resid - alpha * image
        gradient_now = lax.psum(adjoint(resid), ("wide", "narrow"))
        steer = tri_solve(lower, gradient_now, False)
        gamma_new = jnp.sum(steer * steer)
        direction = steer + gamma_new / gamma * direction
        gamma = gamma_new
    return (tri_solve(lower, solved, True), resid, factor)


def solution(mesh):
    return jax.shard_map(
        body,
        mesh=mesh,
        in_specs=(
            P(("wide", "narrow"), None),
            P(("wide", "narrow")),
            P(("wide", "narrow")),
            P(("wide", "narrow")),
            P(),
            P(("wide", "narrow")),
        ),
        out_specs=(P(), P(("wide", "narrow")), P()),
        check_vma=False,
    )
```

profile of v0, /device:TPU:1, one launch (start us, length us, event | category | flops | bytes accessed | tf_op | source)
XLA Modules:
  0.0 1097.9 jit_solution(14000195256907005070)
XLA Ops:
  10.4 7.2 broadcast_multiply_fusion
  25.7 3.9 collective-permute-done
  29.6 4.1 multiply_convert_fusion.2
  33.8 47.2 %collective-permute-done.1 = bf16[2048,512]{1,0:T(8,128)(2,1)} collective-permute-done((bf16[2048,512]{1,0:T(8,128)(2,1)}, bf16[2048,512]{1,0:T(8,128)(2,1)}, u32[]{:S(2)}, u32[]{:S(2)}) %collective-permute-start.1) | collective-permute-done | bytes 2097184 | tf_op jit(solution)/shard_map/ppermute | solution.py:18
  85.4 46.5 %collective-permute-done.2 = bf16[2048,512]{1,0:T(8,128)(2,1)} collective-permute-done((bf16[2048,512]{1,0:T(8,128)(2,1)S(1)}, bf16[2048,512]{1,0:T(8,128)(2,1)}, u32[]{:S(2)}, u32[]{:S(2)}) %collective-permute-start.2) | collective-permute-done | bytes 2097184 | tf_op jit(solution)/shard_map/ppermute | solution.py:18
  131.9 4.1 multiply_convert_fusion
  140.7 79.7 %psum.64 = f32[512,1]{0,1:T(1,128)S(1)} all-reduce(f32[512,1]{0,1:T(1,128)S(1)} %bitcast.533), channel_id=1, replica_groups=mesh['wide'=32,'narrow'=8] {'wide','narrow'}, use_global_device_ids=true, to_apply=%region_10.11 | all-reduce | flops 512 | bytes 4096 | tf_op jit(solution)/shard_map/psum | solution.py:81
  220.5 176.9 %all-reduce.3.cloned.1.call-done = f32[512,512]{0,1:T(8,128)} async-done(((f32[512,512]{0,1:T(8,128)}), f32[512,512]{0,1:T(8,128)}) %all-reduce.3.cloned.1.call-update) | async-done | bytes 1048592 | tf_op jit(solution)/shard_map/psum | solution.py:64
  401.1 11.7 %cholesky.104 = f32[128,128]{1,0:T(8,128)S(1)} custom-call(f32[128,128]{1,0:T(8,128)S(1)} %cholesky.266), custom_call_target="Cholesky" | custom-call | tf_op jit(solution)/shard_map/jit(cholesky)/cholesky | solution.py:67
  412.8 9.8 custom-call.33
  425.3 11.7 %cholesky.217 = f32[128,128]{1,0:T(8,128)S(1)} custom-call(f32[128,128]{1,0:T(8,128)S(1)} %cholesky.270), custom_call_target="Cholesky" | custom-call | tf_op jit(solution)/shard_map/jit(cholesky)/cholesky | solution.py:67
  437.1 10.0 custom-call.34
  448.6 11.7 %cholesky.238 = f32[128,128]{1,0:T(8,128)S(1)} custom-call(f32[128,128]{1,0:T(8,128)S(1)} %cholesky.275), custom_call_target="Cholesky" | custom-call | tf_op jit(solution)/shard_map/jit(cholesky)/cholesky | solution.py:67
  461.1 9.8 custom-call.35
  472.4 11.7 %cholesky.255 = f32[128,128]{1,0:T(8,128)S(1)} custom-call(f32[128,128]{1,0:T(8,128)S(1)} %convolution_subtract_fusion.2), custom_call_target="Cholesky" | custom-call | tf_op jit(solution)/shard_map/jit(cholesky)/cholesky | solution.py:67
  489.5 8.5 while.18
  497.9 39.3 %custom-call.51 = f32[4,128,128]{1,2,0:T(8,128)S(1)} custom-call(f32[4,128,128]{2,1,0:T(8,128)S(1)} %get-tuple-element.71), custom_call_target="InvertDiagBlocksLowerTriangular" | custom-call | tf_op jit(solution)/shard_map/triangular_solve/custom-call.8 | solution.py:32
  542.0 77.5 %psum.65 = f32[]{:T(128)} all-reduce(f32[]{:T(128)} %multiply_reduce_fusion.3), channel_id=1, replica_groups=mesh['wide'=32,'narrow'=8] {'wide','narrow'}, use_global_device_ids=true, to_apply=%region_14.17 | all-reduce | flops 1 | bytes 8 | tf_op jit(solution)/shard_map/psum | solution.py:88
  621.2 73.2 %psum.66 = f32[512,1]{0,1:T(1,128)S(1)} all-reduce(f32[512,1]{0,1:T(1,128)S(1)} %bitcast.534), channel_id=1, replica_groups=mesh['wide'=32,'narrow'=8] {'wide','narrow'}, use_global_device_ids=true, to_apply=%region_15.18 | all-reduce | flops 512 | bytes 4096 | tf_op jit(solution)/shard_map/psum | solution.py:91
  700.4 74.2 %psum.67 = f32[]{:T(128)} all-reduce(f32[]{:T(128)} %multiply_reduce_fusion.2), channel_id=1, replica_groups=mesh['wide'=32,'narrow'=8] {'wide','narrow'}, use_global_device_ids=true, to_apply=%region_19.22 | all-reduce | flops 1 | bytes 8 | tf_op jit(solution)/shard_map/psum | solution.py:88
  776.3 73.4 %psum.68 = f32[512,1]{0,1:T(1,128)S(1)} all-reduce(f32[512,1]{0,1:T(1,128)S(1)} %bitcast.535), channel_id=1, replica_groups=mesh['wide'=32,'narrow'=8] {'wide','narrow'}, use_global_device_ids=true, to_apply=%region_20.23 | all-reduce | flops 512 | bytes 4096 | tf_op jit(solution)/shard_map/psum | solution.py:91
  855.8 74.2 %psum.69 = f32[]{:T(128)} all-reduce(f32[]{:T(128)} %multiply_reduce_fusion.1), channel_id=1, replica_groups=mesh['wide'=32,'narrow'=8] {'wide','narrow'}, use_global_device_ids=true, to_apply=%region_24.27 | all-reduce | flops 1 | bytes 8 | tf_op jit(solution)/shard_map/psum | solution.py:88
  931.7 73.6 %psum.70 = f32[512,1]{0,1:T(1,128)S(1)} all-reduce(f32[512,1]{0,1:T(1,128)S(1)} %bitcast.536), channel_id=1, replica_groups=mesh['wide'=32,'narrow'=8] {'wide','narrow'}, use_global_device_ids=true, to_apply=%region_25.28 | all-reduce | flops 512 | bytes 4096 | tf_op jit(solution)/shard_map/psum | solution.py:91
  1011.3 74.1 %psum.71 = f32[]{:T(128)} all-reduce(f32[]{:T(128)} %multiply_reduce_fusion), channel_id=1, replica_groups=mesh['wide'=32,'narrow'=8] {'wide','narrow'}, use_global_device_ids=true, to_apply=%region_29.32 | all-reduce | flops 1 | bytes 8 | tf_op jit(solution)/shard_map/psum | solution.py:88
  (160 shorter events, 65.6 us)
Async XLA Ops:
  7.2 132.7 %copy-start = (f32[512]{0:T(512)S(1)}, f32[512]{0:T(512)}, u32[]{:S(2)}) copy-start(f32[512]{0:T(512)} %param.14) | copy-start | bytes 6148
  7.2 390.2 %all-reduce.3.cloned.1.call-start = ((), (), s32[]{:S(2)}) async-start(), calls=%async_computation | async-start | bytes 2097152 | tf_op jit(solution)/shard_map/psum | solution.py:64
  22.4 7.2 collective-permute-start
  33.8 47.2 %collective-permute-start.1 = (bf16[2048,512]{1,0:T(8,128)(2,1)}, bf16[2048,512]{1,0:T(8,128)(2,1)}, u32[]{:S(2)}, u32[]{:S(2)}) collective-permute-start(bf16[2048,512]{1,0:T(8,128)(2,1)} %multiply_convert_fusion.2), channel_id=1, source_target_pairs={{0,16},{8,24},{16,0},{24,8},{32,48},{40,56},{48,32},{56,40},{64,80... | collective-permute-start | bytes 6291464 | tf_op jit(solution)/shard_map/ppermute | solution.py:18
  33.8 51.7 %copy-start.6 = (s32[4]{0:T(128)S(1)}, s32[4]{0:T(128)}, u32[]{:S(2)}) copy-start(s32[4]{0:T(128)} %param.13) | copy-start | bytes 52
  84.3 47.6 %collective-permute-start.2 = (bf16[2048,512]{1,0:T(8,128)(2,1)S(1)}, bf16[2048,512]{1,0:T(8,128)(2,1)}, u32[]{:S(2)}, u32[]{:S(2)}) collective-permute-start(bf16[2048,512]{1,0:T(8,128)(2,1)S(1)} %multiply_convert_fusion.1), channel_id=1, source_target_pairs={{0,32},{8,40},{16,48},{24,56},{32,0},{40,8},{48,16},{56,24},{64,96... | collective-permute-start | bytes 6291464 | tf_op jit(solution)/shard_map/ppermute | solution.py:18
  136.0 3.9 copy-start.1
  136.0 3.9 copy-start.4
  136.0 4.4 copy-start.5
  397.4 1.7 copy-start.2
  850.3 237.1 %copy-start.3 = (f32[512,512]{0,1:T(8,128)S(1)}, f32[512,512]{0,1:T(8,128)}, u32[]{:S(2)}) copy-start(f32[512,512]{0,1:T(8,128)} %get-tuple-element.93) | copy-start | bytes 3145732
Sparse Core Ops, SparseCore 0:
  140.0 257.3 all-reduce.2
where the time goes:
time: 1110 us; the launch traced here: 1100 us
  blocking collectives  600 us (54%)
  waiting for transfers between devices  275 us (25%)
  other arithmetic  148 us (13%)
  between operations  26.6 us (2%)
  matrix products  26.4 us (2%)
  local copies, waits for them, and re-layouts  17.4 us (2%)
    psum x4, blocking collectives, body(): alpha = gamma / lax.psum(jnp.sum(image * image), ('wide', 'narrow'))  300 us
    psum x4, blocking collectives, body(): gradient_now = lax.psum(adjoint(resid), ('wide', 'narrow'))  300 us
    psum x1, waiting for transfers between devices, body(): lax.psum(jnp.dot(sketch.T, sketch, preferred_element_type=jnp.float32), (...  177 us
    ppermute x3, waiting for transfers between devices, partner(): return lax.ppermute(value, axis, pairs)  97.6 us
    another operation x14, other arithmetic, body(): lower = jnp.linalg.cholesky(gram)  78.6 us
    another operation x8, other arithmetic, tri_solve(): lax.linalg.triangular_solve(lower, vector[:, None], left_side=True, lower...  40 us
  transfers between devices with their start and end apart: 4, of which 4 were waited for; matrix products, arithmetic and copies ran while one was open for 0% of the time, Pallas kernels for 0%

commit v1 on v0

--- a/solution.py
+++ b/solution.py
@@ -78,7 +78,7 @@
         ).reshape(cols)
 
     resid = apply_design(effects) + noise
-    gradient_now = lax.psum(adjoint(resid), ("wide", "narrow"))
+    gradient_now = jnp.sum(lax.all_gather(adjoint(resid), ("wide", "narrow")), axis=0)
     steer = tri_solve(lower, gradient_now, False)
     direction = steer
     gamma = jnp.sum(steer * steer)

time: 1110 us -> 1110 us (level)
    psum x4 -> x3, blocking collectives: 300 us -> 220 us  [body(): gradient_now = lax.psum(adjoint(resid), ('wide', 'narrow'))]
    all_gather x0 -> x1, blocking collectives: none -> 72.1 us  [body(): lax.all_gather(adjoint(resid), ('wide', 'narrow'))]
where the time goes in v1:
time: 1110 us; the launch traced here: 1100 us
  blocking collectives  592 us (53%)
  waiting for transfers between devices  282 us (25%)
  other arithmetic  149 us (13%)
  between operations  26.5 us (2%)
  matrix products  26.4 us (2%)
  local copies, waits for them, and re-layouts  17.4 us (2%)
    psum x4, blocking collectives, body(): alpha = gamma / lax.psum(jnp.sum(image * image), ('wide', 'narrow'))  300 us
    psum x3, blocking collectives, body(): gradient_now = lax.psum(adjoint(resid), ('wide', 'narrow'))  220 us
    psum x1, waiting for transfers between devices, body(): lax.psum(jnp.dot(sketch.T, sketch, preferred_element_type=jnp.float32), (...  185 us
    ppermute x3, waiting for transfers between devices, partner(): return lax.ppermute(value, axis, pairs)  97 us
    another operation x14, other arithmetic, body(): lower = jnp.linalg.cholesky(gram)  79 us
    all_gather x1, blocking collectives, body(): lax.all_gather(adjoint(resid), ('wide', 'narrow'))  72.1 us
    another operation x8, other arithmetic, tri_solve(): lax.linalg.triangular_solve(lower, vector[:, None], left_side=True, lower...  40 us
  transfers between devices with their start and end apart: 4, of which 4 were waited for; matrix products, arithmetic and copies ran while one was open for 0% of the time, Pallas kernels for 0%

profile of v1, /device:TPU:1, one launch (start us, length us, event | category | flops | bytes accessed | tf_op | source)
XLA Modules:
  0.0 1097.8 jit_solution(13936273339487340898)
XLA Ops:
  10.4 7.2 broadcast_multiply_fusion
  25.7 3.9 collective-permute-done
  29.6 4.1 multiply_convert_fusion.2
  33.8 47.1 %collective-permute-done.1 = bf16[2048,512]{1,0:T(8,128)(2,1)} collective-permute-done((bf16[2048,512]{1,0:T(8,128)(2,1)}, bf16[2048,512]{1,0:T(8,128)(2,1)}, u32[]{:S(2)}, u32[]{:S(2)}) %collective-permute-start.1) | collective-permute-done | bytes 2097184 | tf_op jit(solution)/shard_map/ppermute | solution.py:18
  86.0 45.9 %collective-permute-done.2 = bf16[2048,512]{1,0:T(8,128)(2,1)} collective-permute-done((bf16[2048,512]{1,0:T(8,128)(2,1)S(1)}, bf16[2048,512]{1,0:T(8,128)(2,1)}, u32[]{:S(2)}, u32[]{:S(2)}) %collective-permute-start.2) | collective-permute-done | bytes 2097184 | tf_op jit(solution)/shard_map/ppermute | solution.py:18
  131.9 4.1 multiply_convert_fusion
  140.1 72.1 %all-gather = f32[256,1,512]{2,1,0:T(1,128)S(1)} all-gather(f32[1,1,512]{2,1,0:T(1,128)S(1)} %bitcast.534), channel_id=1, replica_groups=mesh['wide'=32,'narrow'=8] {'wide','narrow'}, dimensions={0}, use_global_device_ids=true | all-gather | bytes 526336 | tf_op jit(solution)/shard_map/all_gather | solution.py:81
  212.5 184.9 %all-reduce.3.cloned.1.call-done = f32[512,512]{0,1:T(8,128)} async-done(((f32[512,512]{0,1:T(8,128)}), f32[512,512]{0,1:T(8,128)}) %all-reduce.3.cloned.1.call-update) | async-done | bytes 1048592 | tf_op jit(solution)/shard_map/psum | solution.py:64
  401.1 11.7 %cholesky.104 = f32[128,128]{1,0:T(8,128)S(1)} custom-call(f32[128,128]{1,0:T(8,128)S(1)} %cholesky.266), custom_call_target="Cholesky" | custom-call | tf_op jit(solution)/shard_map/jit(cholesky)/cholesky | solution.py:67
  413.0 9.8 custom-call.33
  425.3 11.7 %cholesky.217 = f32[128,128]{1,0:T(8,128)S(1)} custom-call(f32[128,128]{1,0:T(8,128)S(1)} %cholesky.270), custom_call_target="Cholesky" | custom-call | tf_op jit(solution)/shard_map/jit(cholesky)/cholesky | solution.py:67
  437.1 10.0 custom-call.34
  448.6 11.7 %cholesky.238 = f32[128,128]{1,0:T(8,128)S(1)} custom-call(f32[128,128]{1,0:T(8,128)S(1)} %cholesky.275), custom_call_target="Cholesky" | custom-call | tf_op jit(solution)/shard_map/jit(cholesky)/cholesky | solution.py:67
  461.1 9.8 custom-call.35
  472.4 12.1 %cholesky.255 = f32[128,128]{1,0:T(8,128)S(1)} custom-call(f32[128,128]{1,0:T(8,128)S(1)} %convolution_subtract_fusion.2), custom_call_target="Cholesky" | custom-call | tf_op jit(solution)/shard_map/jit(cholesky)/cholesky | solution.py:67
  489.5 8.5 while.18
  497.9 39.3 %custom-call.51 = f32[4,128,128]{1,2,0:T(8,128)S(1)} custom-call(f32[4,128,128]{2,1,0:T(8,128)S(1)} %get-tuple-element.71), custom_call_target="InvertDiagBlocksLowerTriangular" | custom-call | tf_op jit(solution)/shard_map/triangular_solve/custom-call.8 | solution.py:32
  542.0 77.5 %psum.57 = f32[]{:T(128)} all-reduce(f32[]{:T(128)} %multiply_reduce_fusion.3), channel_id=1, replica_groups=mesh['wide'=32,'narrow'=8] {'wide','narrow'}, use_global_device_ids=true, to_apply=%region_14.17 | all-reduce | flops 1 | bytes 8 | tf_op jit(solution)/shard_map/psum | solution.py:88
  621.1 73.2 %psum.58 = f32[512,1]{0,1:T(1,128)S(1)} all-reduce(f32[512,1]{0,1:T(1,128)S(1)} %bitcast.539), channel_id=1, replica_groups=mesh['wide'=32,'narrow'=8] {'wide','narrow'}, use_global_device_ids=true, to_apply=%region_15.18 | all-reduce | flops 512 | bytes 4096 | tf_op jit(solution)/shard_map/psum | solution.py:91
  700.4 74.2 %psum.59 = f32[]{:T(128)} all-reduce(f32[]{:T(128)} %multiply_reduce_fusion.2), channel_id=1, replica_groups=mesh['wide'=32,'narrow'=8] {'wide','narrow'}, use_global_device_ids=true, to_apply=%region_19.22 | all-reduce | flops 1 | bytes 8 | tf_op jit(solution)/shard_map/psum | solution.py:88
  776.3 73.4 %psum.60 = f32[512,1]{0,1:T(1,128)S(1)} all-reduce(f32[512,1]{0,1:T(1,128)S(1)} %bitcast.540), channel_id=1, replica_groups=mesh['wide'=32,'narrow'=8] {'wide','narrow'}, use_global_device_ids=true, to_apply=%region_20.23 | all-reduce | flops 512 | bytes 4096 | tf_op jit(solution)/shard_map/psum | solution.py:91
  855.8 74.4 %psum.61 = f32[]{:T(128)} all-reduce(f32[]{:T(128)} %multiply_reduce_fusion.1), channel_id=1, replica_groups=mesh['wide'=32,'narrow'=8] {'wide','narrow'}, use_global_device_ids=true, to_apply=%region_24.27 | all-reduce | flops 1 | bytes 8 | tf_op jit(solution)/shard_map/psum | solution.py:88
  931.9 73.4 %psum.62 = f32[512,1]{0,1:T(1,128)S(1)} all-reduce(f32[512,1]{0,1:T(1,128)S(1)} %bitcast.541), channel_id=1, replica_groups=mesh['wide'=32,'narrow'=8] {'wide','narrow'}, use_global_device_ids=true, to_apply=%region_25.28 | all-reduce | flops 512 | bytes 4096 | tf_op jit(solution)/shard_map/psum | solution.py:91
  1011.3 74.1 %psum.63 = f32[]{:T(128)} all-reduce(f32[]{:T(128)} %multiply_reduce_fusion), channel_id=1, replica_groups=mesh['wide'=32,'narrow'=8] {'wide','narrow'}, use_global_device_ids=true, to_apply=%region_29.32 | all-reduce | flops 1 | bytes 8 | tf_op jit(solution)/shard_map/psum | solution.py:88
  (161 shorter events, 65.5 us)
Async XLA Ops:
  7.2 78.3 %copy-start = (f32[512]{0:T(512)S(1)}, f32[512]{0:T(512)}, u32[]{:S(2)}) copy-start(f32[512]{0:T(512)} %param.14) | copy-start | bytes 6148
  7.2 390.2 %all-reduce.3.cloned.1.call-start = ((), (), s32[]{:S(2)}) async-start(), calls=%async_computation | async-start | bytes 2097152 | tf_op jit(solution)/shard_map/psum | solution.py:64
  22.4 7.2 collective-permute-start
  33.8 47.2 %collective-permute-start.1 = (bf16[2048,512]{1,0:T(8,128)(2,1)}, bf16[2048,512]{1,0:T(8,128)(2,1)}, u32[]{:S(2)}, u32[]{:S(2)}) collective-permute-start(bf16[2048,512]{1,0:T(8,128)(2,1)} %multiply_convert_fusion.2), channel_id=1, source_target_pairs={{0,16},{8,24},{16,0},{24,8},{32,48},{40,56},{48,32},{56,40},{64,80... | collective-permute-start | bytes 6291464 | tf_op jit(solution)/shard_map/ppermute | solution.py:18
  33.8 51.7 %copy-start.1 = (bf16[2048,128]{1,0:T(8,128)(2,1)S(1)}, bf16[2048,128]{1,0:T(8,128)(2,1)}, u32[]{:S(2)}) copy-start(bf16[2048,128]{1,0:T(8,128)(2,1)} %param.10) | copy-start | bytes 1572868
  33.8 51.7 %copy-start.4 = (s32[2048]{0:T(1024)S(1)}, s32[2048]{0:T(1024)}, u32[]{:S(2)}) copy-start(s32[2048]{0:T(1024)} %param.11) | copy-start | bytes 24580
  33.8 52.2 %copy-start.5 = (f32[2048]{0:T(1024)S(1)}, f32[2048]{0:T(1024)}, u32[]{:S(2)}) copy-start(f32[2048]{0:T(1024)} %param.15) | copy-start | bytes 24580
  33.8 52.2 %copy-start.6 = (s32[4]{0:T(128)S(1)}, s32[4]{0:T(128)}, u32[]{:S(2)}) copy-start(s32[4]{0:T(128)} %param.13) | copy-start | bytes 52
  84.3 47.6 %collective-permute-start.2 = (bf16[2048,512]{1,0:T(8,128)(2,1)S(1)}, bf16[2048,512]{1,0:T(8,128)(2,1)}, u32[]{:S(2)}, u32[]{:S(2)}) collective-permute-start(bf16[2048,512]{1,0:T(8,128)(2,1)S(1)} %multiply_convert_fusion.1), channel_id=1, source_target_pairs={{0,32},{8,40},{16,48},{24,56},{32,0},{40,8},{48,16},{56,24},{64,96... | collective-permute-start | bytes 6291464 | tf_op jit(solution)/shard_map/ppermute | solution.py:18
  397.4 1.7 copy-start.2
  853.7 235.8 %copy-start.3 = (f32[512,512]{0,1:T(8,128)S(1)}, f32[512,512]{0,1:T(8,128)}, u32[]{:S(2)}) copy-start(f32[512,512]{0,1:T(8,128)} %get-tuple-element.96) | copy-start | bytes 3145732
Sparse Core Ops, SparseCore 0:
  139.9 257.4 all-reduce.2
